TPU v7x, 32 devices: a whole 2x2x4 slice. The times are simulated.
32 devices in a mesh: freq: 8 (over z, x), panel: 4 (over y, core).
Axes of the slice: x: 2, y: 2, z: 4, core: 2. Of those that a mesh axis runs over, the one named last changes fastest.
Arguments:
- wavefield: float32 [8, 2, 128, 4096], P('freq', None, None, 'panel'), may hold values from -6 to 6
- direct: float32 [8, 2, 128, 4096], P('freq', None, None, 'panel'), may hold values from -6 to 6
- left_factors: float32 [8, 4096, 6, 128], P('freq', 'panel'), may hold values from -0.375 to 0.375
- right_factors: float32 [8, 16, 6, 256, 128], P('freq', 'panel'), may hold values from -0.3125 to 0.3125
- tile_src: int32 [16, 6], P('panel'), may hold values from -1 to 7, as said below
- onset: int32 [128, 2048], P('freq'), may hold values from 128 to 895
Outputs:
- focusing: float32 [8, 2, 128, 4096], P('freq', None, None, 'panel')
Inputs may be any that keep to these rules, and one draw needn't show every extreme that they name: `tile_src`: in each receiver panel's row the first k slots name distinct source tiles, with 2 <= k <= 6, and the other slots hold -1; in every aligned block of 4 panels at least one panel fills all 6 slots.
All inputs are finite; a program needn't handle non-finite values.
Results may differ from a plain program's by a relative error of at most 0.0003.
Values sent between devices are 32-bit elements; how exact they have to be, the bound alone decides.
A program may use at most 128 MiB of HBM per device.

v0:
```python
import functools
import math

import jax
import jax.numpy as jnp
from jax import lax
from jax.experimental import pallas as pl
from jax.experimental.pallas import tpu as pltpu
from jax.sharding import PartitionSpec as P

NT = 1024
FIRST_BIN = 8
SRC_TILES = 8
LANES = 128
BF16 = jnp.bfloat16
F32 = jnp.float32
NN = (((1,), (0,)), ((), ()))
NT_DIMS = (((1,), (1,)), ((), ()))


def split(x):
    high = x.astype(BF16)
    return high, (x - high.astype(F32)).astype(BF16)


def mxu(a, b, dims):
    return lax.dot_general(a, b, dims, preferred_element_type=F32)


def lanes(*parts):
    return jnp.concatenate(parts, axis=1)


def pair_coef(products):
    rows, width = products.shape
    first, second = products[: rows // 2], products[rows // 2 :]
    lane = lax.broadcasted_iota(jnp.int32, first.shape, 1)
    sign = jnp.where(lane < width // 2, 1.0, -1.0).astype(F32)
    swap = lambda x: pltpu.roll(x, width // 2, 1)
    return jnp.concatenate([first + sign * swap(second), second - sign * swap(first)], axis=0)

def gate_tables(count):
    assert 2 * (FIRST_BIN + count - 1) < NT
    cot = lambda m: 1.0 / math.tan(math.pi * m / NT)
    minus = [[0.0 if f == g else cot(g - f) for g in range(count)] for f in range(count)]
    plus = [[cot(f + g + 2 * FIRST_BIN) for g in range(count)] for f in range(count)]
    real = [[0.5 * (minus[f][g] + plus[f][g]) for g in range(count)] for f in range(count)]
    imag = [[0.5 * (plus[f][g] - minus[f][g]) for g in range(count)] for f in range(count)]
    return real, imag


def gate_map(xr, xi, tables):
    real, imag = tables
    count = len(xr)
    total = functools.reduce(lambda a, b: a + b, xr)
    gr, gi = [], []
    for f in range(count):
        a = 0.5 * xr[f] - total
        b = 0.5 * xi[f]
        for g in range(count):
            a = a + real[f][g] * xi[g]
            b = b + imag[f][g] * xr[g]
        gr.append(a)
        gi.append(b)
    return gr, gi


def gate(xr, xi, c1, s1, mark, tables):
    count = len(xr)
    scale = 0.5 / math.sqrt(count * NT)
    ec, es = c1, s1
    power = 1
    while power * 2 <= FIRST_BIN:
        ec, es = ec * ec - es * es, 2.0 * ec * es
        power *= 2
    while power < FIRST_BIN:
        ec, es = ec * c1 - es * s1, ec * s1 + es * c1
        power += 1
    cs, sn = [], []
    for f in range(count):
        cs.append(ec)
        sn.append(es)
        ec, es = ec * c1 - es * s1, ec * s1 + es * c1
    yr = [xr[f] * cs[f] - xi[f] * sn[f] for f in range(count)]
    yi = [xr[f] * sn[f] + xi[f] * cs[f] for f in range(count)]
    hr, hi = gate_map(yr, yi, tables)
    gr, gi = gate_map(xr, xi, tables)
    br = [scale * (cs[f] * hr[f] + sn[f] * hi[f] - gr[f] + mark * xr[f]) for f in range(count)]
    bi = [scale * (cs[f] * hi[f] - sn[f] * hr[f] - gi[f] + mark * xi[f]) for f in range(count)]
    return br, bi


def unit(mark):
    quarter = NT // 4
    phase = mark & (NT - 1)
    quad = lax.shift_right_logical(phase + quarter // 2, quarter.bit_length() - 1)
    x = (2.0 * math.pi / NT) * (phase - quad * quarter).astype(F32)
    z = x * x
    c = jnp.full_like(x, 1.0 / math.factorial(10))
    s = jnp.full_like(x, 1.0 / math.factorial(11))
    for n in (8, 6, 4, 2, 0):
        c = 1.0 / math.factorial(n) - z * c
    for n in (9, 7, 5, 3, 1):
        s = 1.0 / math.factorial(n) - z * s
    s = s * x
    quad = quad & 3
    swap = (quad & 1) == 1
    cos = jnp.where(swap, s, c)
    sin = jnp.where(swap, c, s)
    cos = jnp.where((quad == 1) | (quad == 2), -cos, cos)
    sin = jnp.where(quad >= 2, -sin, sin)
    return cos, sin


def marchenko_kernel(
    nf, ny, chunks, tile_ref, onset_ref, field_hbm, direct_hbm, left_hbm, right_hbm, out_ref,
    field, direct, left, right, coef_h, coef_l, left_h, left_l, right_h, right_l,
    part, buf1, sums, buf2, xbuf, rbuf, obuf, source, chosen_ref,
    field_sem, direct_sem, left_sem, right_sem,
    s1s, s1r, s2s, s2r, s3s, s3r, s4s, s4r, s5s, s5r, s6s, s6r,
):
    tables = gate_tables(nf)
    panels, slots, rows, width = right.shape
    pair = part.shape[1]
    virtual = pair // 2
    vp = virtual // nf
    blocks = rows // LANES
    np_ = 2 * ny
    tiles = np_ // blocks
    me = lax.axis_index("freq")
    q = lax.axis_index("panel")
    y, c = q // 2, q % 2
    partner = {"panel": y * 2 + 1 - c}
    ypeer = [{"panel": ((y + d) % ny) * 2 + c} for d in range(ny)]
    fpeer = [{"freq": (me + d) % nf} for d in range(nf)]
    MESH = pl.DeviceIdType.MESH

    loads_a, loads_b, loads_c = [], [], []
    for p in range(panels):
        cols = pl.ds(p * rows, rows)
        loads_a.append(pltpu.make_async_copy(field_hbm.at[:, :, cols], field.at[p], field_sem.at[p]))
        loads_a.append(pltpu.make_async_copy(left_hbm.at[:, cols, :], left.at[p], left_sem.at[p]))
        loads_b.append(pltpu.make_async_copy(right_hbm.at[p], right.at[p], right_sem.at[p]))
        loads_c.append(pltpu.make_async_copy(direct_hbm.at[:, :, cols], direct.at[p], direct_sem.at[p]))
    for copy in loads_a + loads_b + loads_c:
        copy.start()

    barrier = pltpu.get_barrier_semaphore()
    for dev in [partner] + ypeer[1:] + fpeer[1:]:
        pl.semaphore_signal(barrier, inc=1, device_id=dev, device_id_type=MESH)

    def slot_of(p, j):
        slot = jnp.int32(slots)
        for s in range(slots):
            slot = jnp.where(tile_ref[p, s] == j, jnp.int32(s), slot)
        return slot

    zero = jnp.zeros((pair, width), BF16)
    for p in range(panels):
        coef_h[p, slots] = zero
        coef_l[p, slots] = zero
        left_h[p, slots] = zero[:rows]
        left_l[p, slots] = zero[:rows]

    for p in range(panels):
        loads_a[2 * p].wait()
        loads_a[2 * p + 1].wait()
        fh, fl = split(field[p].reshape(pair, rows))
        fcat = lanes(fh, fh, fl)
        for s in range(0, slots, 2):
            halves = []
            for i in range(2):
                h, l = split(left[p, s + i])
                left_h[p, s + i] = h
                left_l[p, s + i] = l
                halves.append(jnp.concatenate([h, l, h], axis=0))
            products = mxu(fcat, lanes(*halves), NN)
            for i in range(2):
                h, l = split(pair_coef(products[:, i * width : (i + 1) * width]))
                coef_h[p, s + i] = h
                coef_l[p, s + i] = l
    for p in range(panels):
        loads_b[p].wait()
        for s in range(slots):
            h, l = split(right[p, s])
            right_h[p, s] = h
            right_l[p, s] = l

    def send(src, dst, ssem, rsem, device):
        copy = pltpu.make_async_remote_copy(
            src_ref=src, dst_ref=dst, send_sem=ssem, recv_sem=rsem, device_id=device, device_id_type=MESH
        )
        copy.start()
        return copy

    def block(yy, cc, ch):
        return ch * np_ + yy * 2 + cc

    order = list(range(1, ny)) + [0]
    c1 = [[None] * ny for _ in range(chunks)]
    c2 = [[None] * ny for _ in range(chunks)]
    c3 = [[None] * nf for _ in range(chunks)]
    c4 = [[None] * nf for _ in range(chunks)]
    c5 = [[None] * ny for _ in range(chunks)]
    c6 = [[None] * ny for _ in range(chunks)]

    def stage_adjoint(ch):
        for j in range(ch * tiles, (ch + 1) * tiles):
            ins, outs = [], []
            for p in range(panels):
                slot = slot_of(p, j)
                real = jnp.minimum(slot, slots - 1)
                h, l = coef_h[p, slot], coef_l[p, slot]
                rh, rl = right_h[p, real], right_l[p, real]
                ins += [h, l, h]
                outs += [rh, rh, rl]
            tile = mxu(lanes(*ins), lanes(*outs), NT_DIMS)
            for b in range(blocks):
                part[j * blocks + b] = tile[:, b * LANES : (b + 1) * LANES]
        if ch == 0:
            pl.semaphore_wait(barrier, 1 + (ny - 1) + (nf - 1))
        for d in order:
            c1[ch][d] = send(
                part.at[block((y + d) % ny, 1 - c, ch)], buf1.at[ch, d], s1s.at[ch, d], s1r.at[ch, d], partner
            )

    def stage_sum(ch):
        for d in order:
            c1[ch][d].wait_recv()
            sums[ch, d] = part[block((y + d) % ny, c, ch)] + buf1[ch, d]
            if d:
                c2[ch][d] = send(sums.at[ch, d], buf2.at[ch, d - 1], s2s.at[ch, d], s2r.at[ch, d], ypeer[d])

    def stage_out(ch):
        total = sums[ch, 0]
        for d in range(1, ny):
            c2[ch][d].wait_recv()
            total = total + buf2[ch, d - 1]
        if vp % 8 == 0:
            xbuf[ch] = total.reshape(2, nf, vp, LANES)
        else:
            for k in range(2 * nf):
                xbuf[ch, k // nf, k % nf] = total[k * vp : (k + 1) * vp]
        for d in range(1, nf):
            to = (me + d) % nf
            c3[ch][d] = send(xbuf.at[ch, :, to], rbuf.at[ch, me], s3s.at[ch, d], s3r.at[ch, d], fpeer[d])
        rbuf[ch, me] = xbuf[ch, :, me]

    def stage_gate(ch):
        at = block(y, c, ch)
        mark = onset_ref[:, pl.ds(pl.multiple_of(at * LANES, LANES), LANES)]
        cos, sin = unit(mark)
        for d in range(1, nf):
            c3[ch][d].wait_recv()
        xr = [rbuf[ch, f, 0] for f in range(nf)]
        xi = [rbuf[ch, f, 1] for f in range(nf)]
        br, bi = gate(xr, xi, cos, sin, mark.astype(F32), tables)
        for f in range(nf):
            obuf[ch, f, 0] = br[f]
            obuf[ch, f, 1] = bi[f]
        for d in range(1, nf):
            to = (me + d) % nf
            c4[ch][d] = send(obuf.at[ch, to], source.at[at, :, me], s4s.at[ch, d], s4r.at[ch, d], fpeer[d])
        source[at, :, me] = obuf[ch, me]

    def stage_back(ch):
        for d in range(1, nf):
            c4[ch][d].wait_recv()
        at = source.at[block(y, c, ch)]
        for d in range(1, ny):
            c5[ch][d] = send(at, at, s5s.at[ch, d], s5r.at[ch, d], ypeer[d])
        c6[ch][0] = send(at, at, s6s.at[ch, 0], s6r.at[ch, 0], partner)

    def stage_pass(ch):
        for d in range(1, ny):
            c5[ch][d].wait_recv()
            at = source.at[block((y + ny - d) % ny, c, ch)]
            c6[ch][d] = send(at, at, s6s.at[ch, d], s6r.at[ch, d], partner)

    def load_block(b):
        if vp % 8 == 0:
            return source[b].reshape(pair, LANES)
        for k in range(2 * nf):
            chosen_ref[k * vp : (k + 1) * vp, :] = source[b, k // nf, k % nf]
        return chosen_ref[...]

    def forward(ch, d):
        c6[ch][d].wait_recv()
        j = ch * tiles + (y + ny - d) % ny
        h, l = split(lanes(*[load_block(j * blocks + b) for b in range(blocks)]))
        at = [slot_of(p, j) for p in range(panels)]
        real = [jnp.minimum(a, slots - 1) for a in at]
        rh = lanes(*[right_h[p, real[p]] for p in range(panels)])
        rl = lanes(*[right_l[p, real[p]] for p in range(panels)])
        products = mxu(lanes(h, h, l), jnp.concatenate([rh, rl, rh], axis=0), NN)
        for p in range(panels):
            if ch == 0 and d == 0:
                loads_c[p].wait()
            ph, plow = split(pair_coef(products[:, p * width : (p + 1) * width]))
            lh, ll = left_h[p, at[p]], left_l[p, at[p]]
            total = mxu(lanes(ph, ph, plow), lanes(lh, ll, lh), NT_DIMS)
            done = direct[p] - total.reshape(2, virtual, rows)
            if ch == chunks - 1 and d == ny - 1:
                out_ref[:, :, p * rows : (p + 1) * rows] = done
            else:
                direct[p] = done

    def stage_own(ch):
        forward(ch, 0)

    def stage_forward(ch):
        for d in range(1, ny):
            forward(ch, d)

    assert blocks == 2
    for ch in range(chunks):
        stage_adjoint(ch)
        if ch:
            stage_sum(ch - 1)
    stage_sum(chunks - 1)
    stages = [(stage_gate, 2), (stage_out, 0), (stage_back, 3), (stage_pass, 5), (stage_forward, 6), (stage_own, 4)]
    for step in range(chunks + 6):
        for stage, lag in stages:
            if 0 <= step - lag < chunks:
                stage(step - lag)
    for group in (c1, c2, c3, c4, c5, c6):
        for ch in range(chunks):
            for copy in group[ch]:
                if copy is not None:
                    copy.wait_send()


def shards(nf, npanel, wavefield, direct, left_factors, right_factors, tile_src, onset):
    panels, slots = tile_src.shape
    rows, width = right_factors.shape[3:]
    virtual = wavefield.shape[2]
    blocks = SRC_TILES * rows // LANES
    chunks = blocks // npanel
    ny = npanel // 2
    vp = virtual // nf
    pair = 2 * virtual
    left = jnp.transpose(left_factors[0], (1, 0, 2))
    hbm = pl.BlockSpec(memory_space=pl.ANY)
    dma = lambda n: [pltpu.SemaphoreType.DMA((chunks, n))] * 2
    split_buf = lambda n, r: [pltpu.VMEM((panels, n, r, width), BF16)] * 2
    out = pl.pallas_call(
        functools.partial(marchenko_kernel, nf, ny, chunks),
        in_specs=[
            pl.BlockSpec(memory_space=pltpu.SMEM), pl.BlockSpec(memory_space=pltpu.VMEM), hbm, hbm, hbm, hbm,
        ],
        out_specs=pl.BlockSpec(memory_space=pltpu.VMEM),
        out_shape=pltpu.VMEM(direct.shape[1:], F32),
        scratch_shapes=[
            pltpu.VMEM((panels, 2, virtual, rows), F32),
            pltpu.VMEM((panels, 2, virtual, rows), F32),
            pltpu.VMEM((panels, slots, rows, width), F32),
            pltpu.VMEM((panels, slots, rows, width), F32),
            *split_buf(slots + 1, pair),
            *split_buf(slots + 1, rows),
            *split_buf(slots, rows),
            pltpu.VMEM((blocks, pair, LANES), F32),
            pltpu.VMEM((chunks, ny, pair, LANES), F32),
            pltpu.VMEM((chunks, ny, pair, LANES), F32),
            pltpu.VMEM((chunks, ny - 1, pair, LANES), F32),
            pltpu.VMEM((chunks, 2, nf, vp, LANES), F32),
            pltpu.VMEM((chunks, nf, 2, vp, LANES), F32),
            pltpu.VMEM((chunks, nf, 2, vp, LANES), F32),
            pltpu.VMEM((blocks, 2, nf, vp, LANES), F32),
            pltpu.VMEM((pair, LANES), F32),
            *[pltpu.SemaphoreType.DMA((panels,))] * 4,
            *dma(ny), *dma(ny), *dma(nf), *dma(nf), *dma(ny), *dma(ny),
        ],
        compiler_params=pltpu.CompilerParams(collective_id=0, has_side_effects=True),
        name="marchenko",
    )(tile_src, onset, wavefield[0], direct[0], left, right_factors[0])
    return out[None]


def solution(mesh):
    in_specs = (
        P("freq", None, None, "panel"),
        P("freq", None, None, "panel"),
        P("freq", "panel", None, None),
        P("freq", "panel", None, None, None),
        P("panel", None),
        P("freq", None),
    )
    out_specs = P("freq", None, None, "panel")
    body = functools.partial(shards, mesh.shape["freq"], mesh.shape["panel"])
    return jax.shard_map(body, mesh=mesh, in_specs=in_specs, out_specs=out_specs, check_vma=False)
```

profile of v0, /device:TPU:1, one launch (start us, length us, event | category | flops | bytes accessed | tf_op | source)
XLA Modules:
  0.0 48.5 jit_solution(7497728980926485282)
XLA Ops:
  0.0 47.5 %marchenko.1 = f32[2,128,1024]{2,1,0:T(8,128)S(1)} custom-call(s32[4,6]{1,0:T(4,128)} %tile_ref.1, s32[16,2048]{1,0:T(8,128)} %onset_ref.1, f32[2,128,1024]{2,1,0:T(8,128)} %bitcast.10, f32[2,128,1024]{2,1,0:T(8,128)} %bitcast.11, f32[6,1024,128]{2,1,0:T(8,128)} %bitcast.8, f32[4,6,256,128]{3,2,1,0:T(8,128)} %bitcast.9), custom_call_target="tpu_custom_call" | custom-call | tf_op jit(solution)/shard_map/marchenko/pallas_call | solution.py:346
  47.5 1.0 %copy.8 = f32[1,2,128,1024]{3,2,1,0:T(8,128)} copy(f32[1,2,128,1024]{3,2,1,0:T(8,128)S(1)} %bitcast.7) | data formatting | bytes 2097152
where the time goes:
time: 48.6 us; the launch traced here: 48.5 us
  Pallas kernels  47.5 us (98%)
  local copies, waits for them, and re-layouts  0.97 us (2%)
    pallas_call x1, Pallas kernels, shards(): pl.pallas_call(functools.partial(marchenko_kernel, nf, ny, chunks), in_sp...  47.5 us
    unnamed x1, local copies, waits for them, and re-layouts  0.97 us

commit v1 on v0

v1 whole, which is shorter than its diff:
```python
import functools
import math

import jax
import jax.numpy as jnp
from jax import lax
from jax.experimental import pallas as pl
from jax.experimental.pallas import tpu as pltpu
from jax.sharding import PartitionSpec as P

NT = 1024
FIRST_BIN = 8
SRC_TILES = 8
LANES = 128
BF16 = jnp.bfloat16
F32 = jnp.float32
NN = (((1,), (0,)), ((), ()))
NT_DIMS = (((1,), (1,)), ((), ()))


def split(x):
    high = x.astype(BF16)
    return high, (x - high.astype(F32)).astype(BF16)


def mxu(a, b, dims):
    return lax.dot_general(a, b, dims, preferred_element_type=F32)


def lanes(*parts):
    return jnp.concatenate(parts, axis=1)


def pair_coef(products):
    rows, width = products.shape
    first, second = products[: rows // 2], products[rows // 2 :]
    lane = lax.broadcasted_iota(jnp.int32, first.shape, 1)
    sign = jnp.where(lane < width // 2, 1.0, -1.0).astype(F32)
    swap = lambda x: pltpu.roll(x, width // 2, 1)
    return jnp.concatenate([first + sign * swap(second), second - sign * swap(first)], axis=0)

def gate_tables(count):
    assert 2 * (FIRST_BIN + count - 1) < NT
    cot = lambda m: 1.0 / math.tan(math.pi * m / NT)
    minus = [[0.0 if f == g else cot(g - f) for g in range(count)] for f in range(count)]
    plus = [[cot(f + g + 2 * FIRST_BIN) for g in range(count)] for f in range(count)]
    real = [[0.5 * (minus[f][g] + plus[f][g]) for g in range(count)] for f in range(count)]
    imag = [[0.5 * (plus[f][g] - minus[f][g]) for g in range(count)] for f in range(count)]
    return real, imag


def gate_map(xr, xi, tables):
    real, imag = tables
    count = len(xr)
    total = functools.reduce(lambda a, b: a + b, xr)
    gr, gi = [], []
    for f in range(count):
        a = 0.5 * xr[f] - total
        b = 0.5 * xi[f]
        for g in range(count):
            a = a + real[f][g] * xi[g]
            b = b + imag[f][g] * xr[g]
        gr.append(a)
        gi.append(b)
    return gr, gi


def gate(xr, xi, c1, s1, mark, tables):
    count = len(xr)
    scale = 0.5 / math.sqrt(count * NT)
    ec, es = c1, s1
    power = 1
    while power * 2 <= FIRST_BIN:
        ec, es = ec * ec - es * es, 2.0 * ec * es
        power *= 2
    while power < FIRST_BIN:
        ec, es = ec * c1 - es * s1, ec * s1 + es * c1
        power += 1
    cs, sn = [], []
    for f in range(count):
        cs.append(ec)
        sn.append(es)
        ec, es = ec * c1 - es * s1, ec * s1 + es * c1
    yr = [xr[f] * cs[f] - xi[f] * sn[f] for f in range(count)]
    yi = [xr[f] * sn[f] + xi[f] * cs[f] for f in range(count)]
    hr, hi = gate_map(yr, yi, tables)
    gr, gi = gate_map(xr, xi, tables)
    br = [scale * (cs[f] * hr[f] + sn[f] * hi[f] - gr[f] + mark * xr[f]) for f in range(count)]
    bi = [scale * (cs[f] * hi[f] - sn[f] * hr[f] - gi[f] + mark * xi[f]) for f in range(count)]
    return br, bi


def unit(mark):
    quarter = NT // 4
    phase = mark & (NT - 1)
    quad = lax.shift_right_logical(phase + quarter // 2, quarter.bit_length() - 1)
    x = (2.0 * math.pi / NT) * (phase - quad * quarter).astype(F32)
    z = x * x
    c = jnp.full_like(x, 1.0 / math.factorial(10))
    s = jnp.full_like(x, 1.0 / math.factorial(11))
    for n in (8, 6, 4, 2, 0):
        c = 1.0 / math.factorial(n) - z * c
    for n in (9, 7, 5, 3, 1):
        s = 1.0 / math.factorial(n) - z * s
    s = s * x
    quad = quad & 3
    swap = (quad & 1) == 1
    cos = jnp.where(swap, s, c)
    sin = jnp.where(swap, c, s)
    cos = jnp.where((quad == 1) | (quad == 2), -cos, cos)
    sin = jnp.where(quad >= 2, -sin, sin)
    return cos, sin


def halves_of(vp):
    return 2 if vp % 16 == 0 else 1


def marchenko_kernel(
    nf, ny, chunks, tile_hbm, onset_hbm, field_hbm, direct_hbm, left_hbm, right_hbm, out_ref,
    tile_ref, onset_ref, field, direct, left, right, fcat, left_h, left_l, right_h, right_l,
    part, buf1, sums, buf2, xbuf, rbuf, obuf, source, chosen_ref,
    tile_sem, onset_sem, field_sem, direct_sem, left_sem, right_sem,
    s1s, s1r, s2s, s2r, s3s, s3r, s4s, s4r, s5s, s5r, s6s, s6r,
):
    tables = gate_tables(nf)
    panels, slots, rows, width = right.shape
    parts, prow = part.shape[3:5]
    pair = parts * prow
    virtual = pair // 2
    vp = virtual // nf
    vh = vp // parts
    aligned = vh % 8 == 0
    blocks = rows // LANES
    np_ = 2 * ny
    tiles = np_ // blocks
    steps = chunks * parts
    me = lax.axis_index("freq")
    q = lax.axis_index("panel")
    y, c = q // 2, q % 2
    partner = {"panel": y * 2 + 1 - c}
    ypeer = [{"panel": ((y + d) % ny) * 2 + c} for d in range(ny)]
    fpeer = [{"freq": (me + d) % nf} for d in range(nf)]
    MESH = pl.DeviceIdType.MESH

    tile_load = pltpu.make_async_copy(tile_hbm, tile_ref, tile_sem)
    onset_load = pltpu.make_async_copy(onset_hbm, onset_ref, onset_sem)
    loads_a, loads_b, loads_c = [], [], []
    for p in range(panels):
        cols = pl.ds(p * rows, rows)
        if aligned:
            group = [
                pltpu.make_async_copy(field_hbm.at[:, :, h, :, cols], field.at[p, h], field_sem.at[p])
                for h in range(parts)
            ]
            for h in range(parts):
                loads_c.append(
                    pltpu.make_async_copy(direct_hbm.at[:, :, h, :, cols], direct.at[p, h], direct_sem)
                )
        else:
            group = [pltpu.make_async_copy(field_hbm.at[:, :, cols], field.at[p], field_sem.at[p])]
            loads_c.append(pltpu.make_async_copy(direct_hbm.at[:, :, cols], direct.at[p], direct_sem))
        group.append(pltpu.make_async_copy(left_hbm.at[:, cols, :], left[p], left_sem.at[p]))
        loads_a.append(group)
        loads_b.append(pltpu.make_async_copy(right_hbm.at[p], right.at[p], right_sem))
    tile_load.start()
    for group in loads_a:
        for copy in group:
            copy.start()
    for copy in loads_b + [onset_load] + loads_c:
        copy.start()

    barrier = pltpu.get_barrier_semaphore()
    for dev in [partner] + ypeer[1:] + fpeer[1:]:
        pl.semaphore_signal(barrier, inc=1, device_id=dev, device_id_type=MESH)

    tile_load.wait()

    def arrived(ref, sem):
        pltpu.make_async_copy(ref, ref, sem).wait()

    def slot_of(p, j):
        slot = jnp.int32(0)
        live = jnp.int32(0)
        for s in range(slots):
            hit = tile_ref[p, s] == j
            slot = jnp.where(hit, jnp.int32(s), slot)
            live = jnp.where(hit, jnp.int32(1), live)
        return slot, live.astype(F32)

    def send(src, dst, ssem, rsem, device):
        copy = pltpu.make_async_remote_copy(
            src_ref=src, dst_ref=dst, send_sem=ssem, recv_sem=rsem, device_id=device, device_id_type=MESH
        )
        copy.start()

    def coef_of(products):
        return jnp.concatenate([pair_coef(products[h * prow : (h + 1) * prow]) for h in range(parts)], axis=0)

    def block(yy, cc, ch):
        return ch * np_ + yy * 2 + cc

    order = list(range(1, ny)) + [0]

    def stage_adjoint(ch):
        first = ch * tiles
        found = [[slot_of(p, first + t) for t in range(tiles)] for p in range(panels)]
        coefs = [[None] * panels for _ in range(tiles)]
        for p in range(panels):
            if ch == 0:
                arrived(field.at[p], field_sem.at[p])
                arrived(left[p], left_sem.at[p])
                fh, fl = split(field[p].reshape(pair, rows))
                fcat[p, :, :rows] = fh
                fcat[p, :, rows : 2 * rows] = fh
                fcat[p, :, 2 * rows :] = fl
            for t0 in range(0, tiles, 2):
                sides = []
                for t in range(t0, min(t0 + 2, tiles)):
                    slot, live = found[p][t]
                    h, l = split(left[p][slot] * live)
                    left_h[p, first + t] = h
                    left_l[p, first + t] = l
                    sides.append(jnp.concatenate([h, l, h], axis=0))
                products = mxu(fcat[p], lanes(*sides), NN)
                for i in range(len(sides)):
                    coefs[t0 + i][p] = split(coef_of(products[:, i * width : (i + 1) * width]))
        for t in range(tiles):
            ins, outs = [], []
            for p in range(panels):
                if ch == 0 and t == 0 and p == 0:
                    arrived(right, right_sem)
                rh, rl = split(right[p, found[p][t][0]])
                right_h[p, first + t] = rh
                right_l[p, first + t] = rl
                h, l = coefs[t][p]
                ins += [h, l, h]
                outs += [rh, rh, rl]
            tile = mxu(lanes(*ins), lanes(*outs), NT_DIMS)
            for b in range(blocks):
                for h in range(parts):
                    part[ch, t, b, h] = tile[h * prow : (h + 1) * prow, b * LANES : (b + 1) * LANES]
        if ch == 0:
            pl.semaphore_wait(barrier, 1 + (ny - 1) + (nf - 1))
        for h in range(parts):
            k = ch * parts + h
            send(part.at[ch, :, 1 - c, h], buf1.at[k], s1s, s1r.at[k], partner)

    def stage_sum(k):
        ch, h = divmod(k, parts)
        arrived(buf1.at[k], s1r.at[k])
        for d in order:
            yy = (y + d) % ny
            sums[k, d] = part[ch, yy, c, h] + buf1[k, yy]
            if d:
                send(sums.at[k, d], buf2.at[k, d - 1], s2s, s2r.at[k], ypeer[d])

    def stage_out(k):
        total = sums[k, 0]
        arrived(buf2.at[k], s2r.at[k])
        for d in range(1, ny):
            total = total + buf2[k, d - 1]
        if aligned:
            xbuf[k] = total.reshape(2, nf, vh, LANES)
        else:
            for i in range(2 * nf):
                xbuf[k, i // nf, i % nf] = total[i * vh : (i + 1) * vh]
        for d in range(1, nf):
            to = (me + d) % nf
            send(xbuf.at[k, :, to], rbuf.at[k, me], s3s, s3r.at[k], fpeer[d])
        rbuf[k, me] = xbuf[k, :, me]

    def stage_gate(k):
        ch, h = divmod(k, parts)
        at = block(y, c, ch)
        if k == 0:
            onset_load.wait()
        mark = onset_ref[h * vh : (h + 1) * vh, pl.ds(pl.multiple_of(at * LANES, LANES), LANES)]
        cos, sin = unit(mark)
        arrived(rbuf.at[k, : nf - 1], s3r.at[k])
        xr = [rbuf[k, f, 0] for f in range(nf)]
        xi = [rbuf[k, f, 1] for f in range(nf)]
        br, bi = gate(xr, xi, cos, sin, mark.astype(F32), tables)
        for f in range(nf):
            obuf[k, f, 0] = br[f]
            obuf[k, f, 1] = bi[f]
        for d in range(1, nf):
            to = (me + d) % nf
            send(obuf.at[k, to], source.at[at, h, :, me], s4s, s4r.at[k], fpeer[d])
        source[at, h, :, me] = obuf[k, me]

    def stage_back(k):
        ch, h = divmod(k, parts)
        arrived(obuf.at[k, : nf - 1], s4r.at[k])
        at = source.at[block(y, c, ch), h]
        for d in range(1, ny):
            send(at, at, s5s, s5r.at[k, d - 1], ypeer[d])
        send(at, at, s6s, s6r.at[ch, 0], partner)

    def stage_pass(k):
        ch, h = divmod(k, parts)
        for d in range(1, ny):
            at = source.at[block((y + ny - d) % ny, c, ch), h]
            arrived(at, s5r.at[k, d - 1])
            send(at, at, s6s, s6r.at[ch, d], partner)

    def load_block(b):
        if aligned:
            return source[b].reshape(pair, LANES)
        for i in range(2 * nf):
            chosen_ref[i * vh : (i + 1) * vh, :] = source[b, 0, i // nf, i % nf]
        return chosen_ref[...]

    seen = []

    def forward(ch, d):
        j = ch * tiles + (y + ny - d) % ny
        arrived(source.at[block((y + ny - d) % ny, 1 - c, ch)], s6r.at[ch, d])
        h, l = split(lanes(*[load_block(j * blocks + b) for b in range(blocks)]))
        rh = lanes(*[right_h[p, j] for p in range(panels)])
        rl = lanes(*[right_l[p, j] for p in range(panels)])
        products = mxu(lanes(h, h, l), jnp.concatenate([rh, rl, rh], axis=0), NN)
        if not seen:
            arrived(direct, direct_sem)
        seen.append((ch, d))
        last = len(seen) == chunks * ny
        for p in range(panels):
            ph, plow = split(coef_of(products[:, p * width : (p + 1) * width]))
            lh, ll = left_h[p, j], left_l[p, j]
            total = mxu(lanes(ph, ph, plow), lanes(lh, ll, lh), NT_DIMS)
            done = direct[p] - total.reshape(direct.shape[1:])
            if not last:
                direct[p] = done
            elif aligned:
                for i in range(parts):
                    out_ref[:, :, i, :, p * rows : (p + 1) * rows] = done[i]
            else:
                out_ref[:, :, p * rows : (p + 1) * rows] = done

    def stage_own(ch):
        forward(ch, 0)

    def stage_forward(ch):
        for d in range(1, ny):
            forward(ch, d)

    assert blocks == 2
    for ch in range(chunks):
        stage_adjoint(ch)
        if ch:
            for h in range(parts):
                stage_sum((ch - 1) * parts + h)
    for h in range(parts):
        stage_sum((chunks - 1) * parts + h)
    for stage, k in schedule(chunks, parts):
        {"out": stage_out, "gate": stage_gate, "back": stage_back, "pass": stage_pass,
         "own": stage_own, "forward": stage_forward}[stage](k)
    arrived(buf1, s1s)
    arrived(buf2, s2s)
    arrived(rbuf.at[:, : nf - 1], s3s)
    arrived(obuf.at[:, : nf - 1], s4s)
    arrived(buf2, s5s)
    arrived(buf1, s6s)


def schedule(chunks, parts):
    steps = chunks * parts
    lags = [("out", 0), ("gate", 4), ("back", 8), ("pass", 10), ("forward", 12), ("own", 9)]
    order = []
    for step in range(2 * steps + 40):
        for stage, lag in lags:
            k = step - lag
            if 0 <= k < steps:
                if stage in ("own", "forward"):
                    if (k + 1) % parts == 0:
                        order.append((stage, k // parts))
                else:
                    order.append((stage, k))
    return order


def shards(nf, npanel, wavefield, direct, left_factors, right_factors, tile_src, onset):
    panels, slots = tile_src.shape
    rows, width = right_factors.shape[3:]
    virtual = wavefield.shape[2]
    blocks = SRC_TILES * rows // LANES
    chunks = blocks // npanel
    ny = npanel // 2
    vp = virtual // nf
    pair = 2 * virtual
    parts = halves_of(vp)
    vh = vp // parts
    steps = chunks * parts
    prow = pair // parts
    left = jnp.transpose(left_factors[0], (1, 0, 2))
    hbm = pl.BlockSpec(memory_space=pl.ANY)
    dma = lambda *n: pltpu.SemaphoreType.DMA(n) if n else pltpu.SemaphoreType.DMA
    split_buf = [pltpu.VMEM((panels, SRC_TILES, rows, width), BF16)] * 2
    if vh % 8 == 0:
        shaped = lambda x: x.reshape(2, nf, parts, vh, x.shape[-1])
        kept = (panels, parts, 2, nf, vh, rows)
    else:
        shaped = lambda x: x
        kept = (panels, 2, virtual, rows)
    field_in, direct_in = shaped(wavefield[0]), shaped(direct[0])
    out = pl.pallas_call(
        functools.partial(marchenko_kernel, nf, ny, chunks),
        in_specs=[hbm] * 6,
        out_specs=pl.BlockSpec(memory_space=pltpu.VMEM),
        out_shape=pltpu.VMEM(direct_in.shape, F32),
        scratch_shapes=[
            pltpu.SMEM(tile_src.shape, jnp.int32),
            pltpu.VMEM(onset.shape, jnp.int32),
            pltpu.VMEM(kept, F32),
            pltpu.VMEM(kept, F32),
            [pltpu.VMEM((slots, rows, width), F32)] * panels,
            pltpu.VMEM((panels, slots, rows, width), F32),
            pltpu.VMEM((panels, pair, 3 * rows), BF16),
            *split_buf,
            *split_buf,
            pltpu.VMEM((chunks, ny, 2, parts, prow, LANES), F32),
            pltpu.VMEM((steps, ny, prow, LANES), F32),
            pltpu.VMEM((steps, ny, prow, LANES), F32),
            pltpu.VMEM((steps, ny - 1, prow, LANES), F32),
            pltpu.VMEM((steps, 2, nf, vh, LANES), F32),
            pltpu.VMEM((steps, nf, 2, vh, LANES), F32),
            pltpu.VMEM((steps, nf, 2, vh, LANES), F32),
            pltpu.VMEM((blocks, parts, 2, nf, vh, LANES), F32),
            pltpu.VMEM((pair, LANES), F32),
            dma(), dma(),
            dma(panels), dma(), dma(panels), dma(),
            dma(), dma(steps), dma(), dma(steps), dma(), dma(steps),
            dma(), dma(steps), dma(), dma(steps, ny - 1), dma(), dma(chunks, ny),
        ],
        compiler_params=pltpu.CompilerParams(collective_id=0, has_side_effects=True),
        name="marchenko",
    )(tile_src, onset, field_in, direct_in, left, right_factors[0])
    return out.reshape(direct.shape)


def solution(mesh):
    in_specs = (
        P("freq", None, None, "panel"),
        P("freq", None, None, "panel"),
        P("freq", "panel", None, None),
        P("freq", "panel", None, None, None),
        P("panel", None),
        P("freq", None),
    )
    out_specs = P("freq", None, None, "panel")
    body = functools.partial(shards, mesh.shape["freq"], mesh.shape["panel"])
    return jax.shard_map(body, mesh=mesh, in_specs=in_specs, out_specs=out_specs, check_vma=False)
```

time: 48.6 us -> 46.6 us (0.959)
  Pallas kernels: 47.5 us -> 45.4 us
    pallas_call x1, Pallas kernels: 47.5 us -> 45.4 us  [shards(): pl.pallas_call(functools.partial(marchenko_kernel, nf, ny, chunks), in_sp...]
where the time goes in v1:
time: 46.6 us; the launch traced here: 46.4 us
  Pallas kernels  45.4 us (97%)
  local copies, waits for them, and re-layouts  0.97 us (2%)
    pallas_call x1, Pallas kernels, shards(): pl.pallas_call(functools.partial(marchenko_kernel, nf, ny, chunks), in_sp...  45.4 us
    unnamed x1, local copies, waits for them, and re-layouts  0.97 us

profile of v1, /device:TPU:1, one launch (start us, length us, event | category | flops | bytes accessed | tf_op | source)
XLA Modules:
  0.0 46.4 jit_solution(3960548069890673065)
XLA Ops:
  0.0 45.4 %marchenko.1 = f32[2,8,2,8,1024]{4,3,2,1,0:T(8,128)S(1)} custom-call(s32[4,6]{1,0:T(4,128)} %tile_hbm.1, s32[16,2048]{1,0:T(8,128)} %onset_hbm.1, f32[2,8,2,8,1024]{4,3,2,1,0:T(8,128)} %bitcast.10, f32[2,8,2,8,1024]{4,3,2,1,0:T(8,128)} %bitcast.11, f32[6,1024,128]{2,1,0:T(8,128)} %bitcast.8, f32[4,6,256,128]{3,2,1,0:T(8,128)} %bitcast.9), custom_call_target="tpu_custom_call" | custom-call | tf_op jit(solution)/shard_map/marchenko/pallas_call | solution.py:406
  45.4 1.0 %copy.8 = f32[1,2,128,1024]{3,2,1,0:T(8,128)} copy(f32[1,2,128,1024]{3,2,1,0:T(8,128)S(1)} %bitcast.7) | data formatting | bytes 2097152

commit v2 on v1

--- a/solution.py
+++ b/solution.py
@@ -119,9 +119,9 @@
 def marchenko_kernel(
     nf, ny, chunks, tile_hbm, onset_hbm, field_hbm, direct_hbm, left_hbm, right_hbm, out_ref,
     tile_ref, onset_ref, field, direct, left, right, fcat, left_h, left_l, right_h, right_l,
-    part, buf1, sums, buf2, xbuf, rbuf, obuf, source, chosen_ref,
+    part, buf1, sums, buf2, xbuf, rbuf, obuf, source, chosen_ref, xfirst, rfirst, yfirst, ylast,
     tile_sem, onset_sem, field_sem, direct_sem, left_sem, right_sem,
-    s1s, s1r, s2s, s2r, s3s, s3r, s4s, s4r, s5s, s5r, s6s, s6r,
+    s1s, s1r, s2s, s2r, s3s, s3r, s4s, s4r, s5s, s5r, s6s, s6r, s7s, s7r, s8s, s8r,
 ):
     tables = gate_tables(nf)
     panels, slots, rows, width = right.shape
@@ -135,6 +135,7 @@
     np_ = 2 * ny
     tiles = np_ // blocks
     steps = chunks * parts
+    early = late = int(ny == 2)
     me = lax.axis_index("freq")
     q = lax.axis_index("panel")
     y, c = q // 2, q % 2
@@ -167,14 +168,10 @@
     for group in loads_a:
         for copy in group:
             copy.start()
-    for copy in loads_b + [onset_load] + loads_c:
-        copy.start()
 
     barrier = pltpu.get_barrier_semaphore()
     for dev in [partner] + ypeer[1:] + fpeer[1:]:
         pl.semaphore_signal(barrier, inc=1, device_id=dev, device_id_type=MESH)
-
-    tile_load.wait()
 
     def arrived(ref, sem):
         pltpu.make_async_copy(ref, ref, sem).wait()
@@ -195,21 +192,39 @@
         copy.start()
 
     def coef_of(products):
-        return jnp.concatenate([pair_coef(products[h * prow : (h + 1) * prow]) for h in range(parts)], axis=0)
+        count = products.shape[0] // prow
+        return jnp.concatenate([pair_coef(products[h * prow : (h + 1) * prow]) for h in range(count)], axis=0)
 
     def block(yy, cc, ch):
         return ch * np_ + yy * 2 + cc
 
     order = list(range(1, ny)) + [0]
+    half = prow // 2
+    whole = [(slice(0, 2), 0)]
+
+    def lines(i):
+        return slice(0, prow) if isinstance(i, slice) else slice(i * half, (i + 1) * half)
+
+    def entering(k):
+        return [(0, 0), (1, steps - k)] if k == early else whole
+
+    def leaving(k):
+        return [(i, i) for i in range(2)] if k == steps - 1 and not late else whole
+
 
     def stage_adjoint(ch):
         first = ch * tiles
+        if ch == 0:
+            tile_load.wait()
         found = [[slot_of(p, first + t) for t in range(tiles)] for p in range(panels)]
         coefs = [[None] * panels for _ in range(tiles)]
         for p in range(panels):
             if ch == 0:
                 arrived(field.at[p], field_sem.at[p])
                 arrived(left[p], left_sem.at[p])
+                if p == min(1, panels - 1):
+                    for copy in loads_b:
+                        copy.start()
                 fh, fl = split(field[p].reshape(pair, rows))
                 fcat[p, :, :rows] = fh
                 fcat[p, :, rows : 2 * rows] = fh
@@ -241,6 +256,8 @@
                 for h in range(parts):
                     part[ch, t, b, h] = tile[h * prow : (h + 1) * prow, b * LANES : (b + 1) * LANES]
         if ch == 0:
+            for copy in [onset_load] + loads_c:
+                copy.start()
             pl.semaphore_wait(barrier, 1 + (ny - 1) + (nf - 1))
         for h in range(parts):
             k = ch * parts + h
@@ -249,134 +266,213 @@
     def stage_sum(k):
         ch, h = divmod(k, parts)
         arrived(buf1.at[k], s1r.at[k])
+        if k < early:
+            for d in range(ny):
+                yy = (y + d) % ny
+                spread(xfirst.at[d], part[ch, yy, c, h] + buf1[k, yy], 0)
+            for d in range(1, nf):
+                to = (me + d) % nf
+                send(xfirst.at[:, :, to], rfirst.at[:, me], s7s, s7r, fpeer[d])
+            rfirst[:, me] = xfirst[:, :, me]
+            return
         for d in order:
             yy = (y + d) % ny
             sums[k, d] = part[ch, yy, c, h] + buf1[k, yy]
             if d:
-                send(sums.at[k, d], buf2.at[k, d - 1], s2s, s2r.at[k], ypeer[d])
+                for i, at in entering(k):
+                    send(sums.at[k, d, lines(i)], buf2.at[k, d - 1, lines(i)], s2s, s2r.at[k + at], ypeer[d])
+
+    def spread(ref, total, first):
+        for r in range(total.shape[0] // vh):
+            ref[first + r // nf, r % nf] = total[r * vh : (r + 1) * vh]
 
     def stage_out(k):
-        total = sums[k, 0]
-        arrived(buf2.at[k], s2r.at[k])
-        for d in range(1, ny):
-            total = total + buf2[k, d - 1]
-        if aligned:
-            xbuf[k] = total.reshape(2, nf, vh, LANES)
-        else:
-            for i in range(2 * nf):
-                xbuf[k, i // nf, i % nf] = total[i * vh : (i + 1) * vh]
-        for d in range(1, nf):
-            to = (me + d) % nf
-            send(xbuf.at[k, :, to], rbuf.at[k, me], s3s, s3r.at[k], fpeer[d])
+        if k < early:
+            arrived(rfirst.at[:, : nf - 1], s7r)
+            for d in range(1, ny):
+                send(rfirst.at[d], yfirst.at[d - 1], s2s, s2r.at[k], ypeer[d])
+            return
+        for i, at in entering(k):
+            total = sums[k, 0, lines(i)]
+            arrived(buf2.at[k, :, lines(i)], s2r.at[k + at])
+            for d in range(1, ny):
+                total = total + buf2[k, d - 1, lines(i)]
+            spread(xbuf.at[k], total, 0 if isinstance(i, slice) else i)
+            for d in range(1, nf):
+                to = (me + d) % nf
+                send(xbuf.at[k, i, to], rbuf.at[k, me, i], s3s, s3r.at[k], fpeer[d])
         rbuf[k, me] = xbuf[k, :, me]
 
     def stage_gate(k):
         ch, h = divmod(k, parts)
         at = block(y, c, ch)
-        if k == 0:
+        if not gates:
             onset_load.wait()
+        gates.append(k)
         mark = onset_ref[h * vh : (h + 1) * vh, pl.ds(pl.multiple_of(at * LANES, LANES), LANES)]
         cos, sin = unit(mark)
-        arrived(rbuf.at[k, : nf - 1], s3r.at[k])
-        xr = [rbuf[k, f, 0] for f in range(nf)]
-        xi = [rbuf[k, f, 1] for f in range(nf)]
+        if k < early:
+            arrived(yfirst, s2r.at[k])
+            both = [[rfirst[0, f, i] for f in range(nf)] for i in range(2)]
+            for d in range(1, ny):
+                both = [[both[i][f] + yfirst[d - 1, f, i] for f in range(nf)] for i in range(2)]
+            xr, xi = both
+        else:
+            arrived(rbuf.at[k, : nf - 1], s3r.at[k])
+            xr = [rbuf[k, f, 0] for f in range(nf)]
+            xi = [rbuf[k, f, 1] for f in range(nf)]
         br, bi = gate(xr, xi, cos, sin, mark.astype(F32), tables)
         for f in range(nf):
             obuf[k, f, 0] = br[f]
             obuf[k, f, 1] = bi[f]
-        for d in range(1, nf):
-            to = (me + d) % nf
-            send(obuf.at[k, to], source.at[at, h, :, me], s4s, s4r.at[k], fpeer[d])
+        for i, sem in leaving(k):
+            for d in range(1, nf):
+                to = (me + d) % nf
+                send(obuf.at[k, to, i], source.at[at, h, i, me], s4s, s4r.at[k + sem], fpeer[d])
         source[at, h, :, me] = obuf[k, me]
+        if k >= steps - late:
+            for d in range(1, ny):
+                send(obuf.at[k], ylast.at[d - 1], s5s, s5r.at[k, d - 1], ypeer[d])
+
+    def stage_cross(k):
+        ch, h = divmod(k, parts)
+        for d in range(1, ny):
+            arrived(ylast.at[d - 1], s5r.at[k, d - 1])
+            there = block((y + ny - d) % ny, c, ch)
+            for e in range(1, nf):
+                to = (me + e) % nf
+                send(ylast.at[d - 1, to], source.at[there, h, :, me], s8s, s8r.at[d - 1], fpeer[e])
+            source[there, h, :, me] = ylast[d - 1, me]
 
     def stage_back(k):
         ch, h = divmod(k, parts)
-        arrived(obuf.at[k, : nf - 1], s4r.at[k])
-        at = source.at[block(y, c, ch), h]
-        for d in range(1, ny):
-            send(at, at, s5s, s5r.at[k, d - 1], ypeer[d])
-        send(at, at, s6s, s6r.at[ch, 0], partner)
+        for i, sem in leaving(k):
+            arrived(obuf.at[k, : nf - 1, i], s4r.at[k + sem])
+            at = source.at[block(y, c, ch), h, i]
+            if k < steps - late:
+                for d in range(1, ny):
+                    send(at, at, s5s, s5r.at[k + sem, d - 1], ypeer[d])
+            send(at, at, s6s, s6r.at[lot(k), 0], partner)
 
     def stage_pass(k):
         ch, h = divmod(k, parts)
-        for d in range(1, ny):
-            at = source.at[block((y + ny - d) % ny, c, ch), h]
-            arrived(at, s5r.at[k, d - 1])
-            send(at, at, s6s, s6r.at[ch, d], partner)
-
-    def load_block(b):
+        for i, sem in leaving(k):
+            for d in range(1, ny):
+                at = source.at[block((y + ny - d) % ny, c, ch), h, i]
+                if k < steps - late:
+                    arrived(at, s5r.at[k + sem, d - 1])
+                else:
+                    arrived(obuf.at[k, : nf - 1], s8r.at[d - 1])
+                send(at, at, s6s, s6r.at[lot(k), d], partner)
+
+    def lot(k):
+        return k // parts if k < (chunks - 1) * parts else chunks - 1 + k % parts
+
+    def load_block(b, hs):
         if aligned:
-            return source[b].reshape(pair, LANES)
+            return source[b, hs[0] : hs[-1] + 1].reshape(len(hs) * prow, LANES)
         for i in range(2 * nf):
             chosen_ref[i * vh : (i + 1) * vh, :] = source[b, 0, i // nf, i % nf]
         return chosen_ref[...]
 
-    seen = []
-
-    def forward(ch, d):
+    seen = [0] * parts
+    gates = []
+
+    def forward(ch, d, hs):
         j = ch * tiles + (y + ny - d) % ny
-        arrived(source.at[block((y + ny - d) % ny, 1 - c, ch)], s6r.at[ch, d])
-        h, l = split(lanes(*[load_block(j * blocks + b) for b in range(blocks)]))
+        there = block((y + ny - d) % ny, 1 - c, ch)
+        if ch < chunks - 1:
+            arrived(source.at[there], s6r.at[ch, d])
+        else:
+            for i in hs:
+                arrived(source.at[there, i], s6r.at[ch + i, d])
+        h, l = split(lanes(*[load_block(j * blocks + b, hs) for b in range(blocks)]))
         rh = lanes(*[right_h[p, j] for p in range(panels)])
         rl = lanes(*[right_l[p, j] for p in range(panels)])
         products = mxu(lanes(h, h, l), jnp.concatenate([rh, rl, rh], axis=0), NN)
-        if not seen:
+        if not any(seen):
             arrived(direct, direct_sem)
-        seen.append((ch, d))
-        last = len(seen) == chunks * ny
+        for i in hs:
+            seen[i] += 1
         for p in range(panels):
             ph, plow = split(coef_of(products[:, p * width : (p + 1) * width]))
             lh, ll = left_h[p, j], left_l[p, j]
             total = mxu(lanes(ph, ph, plow), lanes(lh, ll, lh), NT_DIMS)
-            done = direct[p] - total.reshape(direct.shape[1:])
-            if not last:
-                direct[p] = done
-            elif aligned:
-                for i in range(parts):
-                    out_ref[:, :, i, :, p * rows : (p + 1) * rows] = done[i]
-            else:
-                out_ref[:, :, p * rows : (p + 1) * rows] = done
-
-    def stage_own(ch):
-        forward(ch, 0)
-
-    def stage_forward(ch):
+            for n, i in enumerate(hs):
+                mine = total[n * prow : (n + 1) * prow]
+                if not aligned:
+                    done = direct[p] - mine.reshape(direct.shape[1:])
+                    if seen[i] == chunks * ny:
+                        out_ref[:, :, p * rows : (p + 1) * rows] = done
+                    else:
+                        direct[p] = done
+                else:
+                    done = direct[p, i] - mine.reshape(direct.shape[2:])
+                    if seen[i] == chunks * ny:
+                        out_ref[:, :, i, :, p * rows : (p + 1) * rows] = done
+                    else:
+                        direct[p, i] = done
+
+    def stage_own(k):
+        forward(k // parts, 0, list(range(parts)))
+
+    def stage_forward(k):
         for d in range(1, ny):
-            forward(ch, d)
+            forward(k // parts, d, list(range(parts)))
+
+    def stage_near(k):
+        forward(k // parts, 0, [k % parts])
+
+    def stage_far(k):
+        for d in range(1, ny):
+            forward(k // parts, d, [k % parts])
 
     assert blocks == 2
-    for ch in range(chunks):
-        stage_adjoint(ch)
-        if ch:
-            for h in range(parts):
-                stage_sum((ch - 1) * parts + h)
-    for h in range(parts):
-        stage_sum((chunks - 1) * parts + h)
-    for stage, k in schedule(chunks, parts):
-        {"out": stage_out, "gate": stage_gate, "back": stage_back, "pass": stage_pass,
-         "own": stage_own, "forward": stage_forward}[stage](k)
+    run = {"adjoint": stage_adjoint, "sum": stage_sum, "out": stage_out, "gate": stage_gate, "back": stage_back,
+           "pass": stage_pass, "cross": stage_cross, "own": stage_own, "forward": stage_forward, "near": stage_near, "far": stage_far}
+    for stage, k in schedule(chunks, parts, late):
+        run[stage](k)
     arrived(buf1, s1s)
     arrived(buf2, s2s)
-    arrived(rbuf.at[:, : nf - 1], s3s)
+    arrived(rbuf.at[early:, : nf - 1], s3s)
+    if early:
+        arrived(rfirst.at[:, : nf - 1], s7s)
     arrived(obuf.at[:, : nf - 1], s4s)
     arrived(buf2, s5s)
+    if late:
+        arrived(ylast.at[:, : nf - 1], s8s)
     arrived(buf1, s6s)
 
 
-def schedule(chunks, parts):
+LAGS = {
+    "adjoint": -8, "sum": -5.5, "out": 0, "gate": 2.5, "cross": 5.2, "back": 5.3, "pass": 6.3, "own": 6.4, "forward": 7.4,
+}
+ORDER = [
+    ("adjoint", 0), ("adjoint", 1), ("sum", 0), ("sum", 1), ("sum", 2), ("adjoint", 2), ("sum", 3), ("sum", 4),
+    ("sum", 5), ("out", 1), ("out", 2), ("out", 3), ("out", 0), ("adjoint", 3), ("out", 4), ("sum", 6), ("gate", 1),
+    ("sum", 7), ("out", 5), ("gate", 0), ("out", 6), ("gate", 3), ("out", 7), ("back", 1), ("gate", 2), ("gate", 5),
+    ("gate", 4), ("pass", 1), ("back", 0), ("back", 3), ("own", 1), ("gate", 6), ("gate", 7), ("back", 2),
+    ("back", 5), ("own", 3), ("cross", 7), ("pass", 3), ("back", 4), ("pass", 0), ("back", 6), ("pass", 2),
+    ("own", 5), ("forward", 1), ("back", 7), ("pass", 5), ("forward", 3), ("pass", 4), ("own", 7), ("pass", 7),
+    ("pass", 6), ("forward", 5), ("forward", 7),
+]
+
+
+def schedule(chunks, parts, late):
     steps = chunks * parts
-    lags = [("out", 0), ("gate", 4), ("back", 8), ("pass", 10), ("forward", 12), ("own", 9)]
-    order = []
-    for step in range(2 * steps + 40):
-        for stage, lag in lags:
-            k = step - lag
-            if 0 <= k < steps:
-                if stage in ("own", "forward"):
-                    if (k + 1) % parts == 0:
-                        order.append((stage, k // parts))
-                else:
-                    order.append((stage, k))
-    return order
+    names = ["sum", "out", "gate", "back", "pass"]
+    ops = [("adjoint", ch) for ch in range(chunks)]
+    for k in range(steps):
+        ops += [(name, k) for name in names]
+        if k >= steps - late:
+            ops.append(("cross", k))
+        if k % parts == parts - 1:
+            ops += [("own", k), ("forward", k)]
+    if late and len(ops) == len(ORDER):
+        assert sorted(ops) == sorted(ORDER)
+        return ORDER
+    place = lambda op: LAGS[op[0]] + op[1] * (parts if op[0] == "adjoint" else 1)
+    return sorted(ops, key=place)
 
 
 def shards(nf, npanel, wavefield, direct, left_factors, right_factors, tile_src, onset):
@@ -427,10 +523,15 @@
             pltpu.VMEM((steps, nf, 2, vh, LANES), F32),
             pltpu.VMEM((blocks, parts, 2, nf, vh, LANES), F32),
             pltpu.VMEM((pair, LANES), F32),
+            pltpu.VMEM((ny, 2, nf, vh, LANES), F32),
+            pltpu.VMEM((ny, nf, 2, vh, LANES), F32),
+            pltpu.VMEM((ny - 1, nf, 2, vh, LANES), F32),
+            pltpu.VMEM((ny - 1, nf, 2, vh, LANES), F32),
             dma(), dma(),
             dma(panels), dma(), dma(panels), dma(),
-            dma(), dma(steps), dma(), dma(steps), dma(), dma(steps),
-            dma(), dma(steps), dma(), dma(steps, ny - 1), dma(), dma(chunks, ny),
+            dma(), dma(steps), dma(), dma(steps + 1), dma(), dma(steps),
+            dma(), dma(steps + 1), dma(), dma(steps + 1, ny - 1), dma(), dma(chunks - 1 + parts, ny),
+            dma(), dma(), dma(), dma(ny - 1),
         ],
         compiler_params=pltpu.CompilerParams(collective_id=0, has_side_effects=True),
         name="marchenko",

time: 46.6 us -> 43.6 us (0.936)
  Pallas kernels: 45.4 us -> 42.5 us
    pallas_call x1, Pallas kernels: 45.4 us -> 42.5 us  [shards(): pl.pallas_call(functools.partial(marchenko_kernel, nf, ny, chunks), in_sp...]
where the time goes in v2:
time: 43.6 us; the launch traced here: 43.5 us
  Pallas kernels  42.5 us (97%)
  local copies, waits for them, and re-layouts  0.97 us (2%)
    pallas_call x1, Pallas kernels, shards(): pl.pallas_call(functools.partial(marchenko_kernel, nf, ny, chunks), in_sp...  42.5 us
    unnamed x1, local copies, waits for them, and re-layouts  0.97 us

profile of v2, /device:TPU:1, one launch (start us, length us, event | category | flops | bytes accessed | tf_op | source)
XLA Modules:
  0.0 43.5 jit_solution(10365150799082997307)
XLA Ops:
  0.0 42.5 %marchenko.1 = f32[2,8,2,8,1024]{4,3,2,1,0:T(8,128)S(1)} custom-call(s32[4,6]{1,0:T(4,128)} %tile_hbm.1, s32[16,2048]{1,0:T(8,128)} %onset_hbm.1, f32[2,8,2,8,1024]{4,3,2,1,0:T(8,128)} %bitcast.10, f32[2,8,2,8,1024]{4,3,2,1,0:T(8,128)} %bitcast.11, f32[6,1024,128]{2,1,0:T(8,128)} %bitcast.8, f32[4,6,256,128]{3,2,1,0:T(8,128)} %bitcast.9), custom_call_target="tpu_custom_call" | custom-call | tf_op jit(solution)/shard_map/marchenko/pallas_call | solution.py:502
  42.5 1.0 %copy.8 = f32[1,2,128,1024]{3,2,1,0:T(8,128)} copy(f32[1,2,128,1024]{3,2,1,0:T(8,128)S(1)} %bitcast.7) | data formatting | bytes 2097152

commit v3 on v2

--- a/solution.py
+++ b/solution.py
@@ -117,14 +117,14 @@
 
 
 def marchenko_kernel(
-    nf, ny, chunks, tile_hbm, onset_hbm, field_hbm, direct_hbm, left_hbm, right_hbm, out_ref,
+    nf, ny, chunks, early, late, tile_hbm, onset_hbm, field_hbm, direct_hbm, left_hbm, right_hbm, out_ref,
     tile_ref, onset_ref, field, direct, left, right, fcat, left_h, left_l, right_h, right_l,
     part, buf1, sums, buf2, xbuf, rbuf, obuf, source, chosen_ref, xfirst, rfirst, yfirst, ylast,
     tile_sem, onset_sem, field_sem, direct_sem, left_sem, right_sem,
     s1s, s1r, s2s, s2r, s3s, s3r, s4s, s4r, s5s, s5r, s6s, s6r, s7s, s7r, s8s, s8r,
 ):
     tables = gate_tables(nf)
-    panels, slots, rows, width = right.shape
+    panels, (slots, rows, width) = len(right), right[0].shape
     parts, prow = part.shape[3:5]
     pair = parts * prow
     virtual = pair // 2
@@ -135,7 +135,6 @@
     np_ = 2 * ny
     tiles = np_ // blocks
     steps = chunks * parts
-    early = late = int(ny == 2)
     me = lax.axis_index("freq")
     q = lax.axis_index("panel")
     y, c = q // 2, q % 2
@@ -151,7 +150,7 @@
         cols = pl.ds(p * rows, rows)
         if aligned:
             group = [
-                pltpu.make_async_copy(field_hbm.at[:, :, h, :, cols], field.at[p, h], field_sem.at[p])
+                pltpu.make_async_copy(field_hbm.at[:, :, h, :, cols], field.at[p, h], field_sem)
                 for h in range(parts)
             ]
             for h in range(parts):
@@ -159,15 +158,17 @@
                     pltpu.make_async_copy(direct_hbm.at[:, :, h, :, cols], direct.at[p, h], direct_sem)
                 )
         else:
-            group = [pltpu.make_async_copy(field_hbm.at[:, :, cols], field.at[p], field_sem.at[p])]
+            group = [pltpu.make_async_copy(field_hbm.at[:, :, cols], field.at[p], field_sem)]
             loads_c.append(pltpu.make_async_copy(direct_hbm.at[:, :, cols], direct.at[p], direct_sem))
         group.append(pltpu.make_async_copy(left_hbm.at[:, cols, :], left[p], left_sem.at[p]))
         loads_a.append(group)
-        loads_b.append(pltpu.make_async_copy(right_hbm.at[p], right.at[p], right_sem))
+        loads_b.append(pltpu.make_async_copy(right_hbm.at[p], right[p], right_sem.at[p]))
     tile_load.start()
     for group in loads_a:
-        for copy in group:
+        for copy in group[:-1]:
             copy.start()
+    for group in loads_a:
+        group[-1].start()
 
     barrier = pltpu.get_barrier_semaphore()
     for dev in [partner] + ypeer[1:] + fpeer[1:]:
@@ -216,19 +217,19 @@
         first = ch * tiles
         if ch == 0:
             tile_load.wait()
-        found = [[slot_of(p, first + t) for t in range(tiles)] for p in range(panels)]
-        coefs = [[None] * panels for _ in range(tiles)]
-        for p in range(panels):
-            if ch == 0:
-                arrived(field.at[p], field_sem.at[p])
-                arrived(left[p], left_sem.at[p])
-                if p == min(1, panels - 1):
-                    for copy in loads_b:
-                        copy.start()
+            for copy in loads_b:
+                copy.start()
+            arrived(field, field_sem)
+            for p in range(panels):
                 fh, fl = split(field[p].reshape(pair, rows))
                 fcat[p, :, :rows] = fh
                 fcat[p, :, rows : 2 * rows] = fh
                 fcat[p, :, 2 * rows :] = fl
+            for p in range(panels):
+                arrived(left[p], left_sem.at[p])
+        found = [[slot_of(p, first + t) for t in range(tiles)] for p in range(panels)]
+        coefs = [[None] * panels for _ in range(tiles)]
+        for p in range(panels):
             for t0 in range(0, tiles, 2):
                 sides = []
                 for t in range(t0, min(t0 + 2, tiles)):
@@ -240,18 +241,23 @@
                 products = mxu(fcat[p], lanes(*sides), NN)
                 for i in range(len(sides)):
                     coefs[t0 + i][p] = split(coef_of(products[:, i * width : (i + 1) * width]))
-        for t in range(tiles):
-            ins, outs = [], []
-            for p in range(panels):
-                if ch == 0 and t == 0 and p == 0:
-                    arrived(right, right_sem)
-                rh, rl = split(right[p, found[p][t][0]])
-                right_h[p, first + t] = rh
-                right_l[p, first + t] = rl
-                h, l = coefs[t][p]
-                ins += [h, l, h]
-                outs += [rh, rh, rl]
-            tile = mxu(lanes(*ins), lanes(*outs), NT_DIMS)
+        step = (panels + 1) // 2 if ch == 0 else panels
+        sums_t = [None] * tiles
+        for p0 in range(0, panels, step):
+            for t in range(tiles):
+                ins, outs = [], []
+                for p in range(p0, min(p0 + step, panels)):
+                    if ch == 0 and t == 0:
+                        arrived(right[p], right_sem.at[p])
+                    rh, rl = split(right[p][found[p][t][0]])
+                    right_h[p, first + t] = rh
+                    right_l[p, first + t] = rl
+                    h, l = coefs[t][p]
+                    ins += [h, l, h]
+                    outs += [rh, rh, rl]
+                more = mxu(lanes(*ins), lanes(*outs), NT_DIMS)
+                sums_t[t] = more if p0 == 0 else sums_t[t] + more
+        for t, tile in enumerate(sums_t):
             for b in range(blocks):
                 for h in range(parts):
                     part[ch, t, b, h] = tile[h * prow : (h + 1) * prow, b * LANES : (b + 1) * LANES]
@@ -269,11 +275,11 @@
         if k < early:
             for d in range(ny):
                 yy = (y + d) % ny
-                spread(xfirst.at[d], part[ch, yy, c, h] + buf1[k, yy], 0)
+                spread(xfirst.at[k, d], part[ch, yy, c, h] + buf1[k, yy], 0)
             for d in range(1, nf):
                 to = (me + d) % nf
-                send(xfirst.at[:, :, to], rfirst.at[:, me], s7s, s7r, fpeer[d])
-            rfirst[:, me] = xfirst[:, :, me]
+                send(xfirst.at[k, :, :, to], rfirst.at[k, :, me], s7s, s7r.at[k], fpeer[d])
+            rfirst[k, :, me] = xfirst[k, :, :, me]
             return
         for d in order:
             yy = (y + d) % ny
@@ -288,9 +294,9 @@
 
     def stage_out(k):
         if k < early:
-            arrived(rfirst.at[:, : nf - 1], s7r)
+            arrived(rfirst.at[k, :, : nf - 1], s7r.at[k])
             for d in range(1, ny):
-                send(rfirst.at[d], yfirst.at[d - 1], s2s, s2r.at[k], ypeer[d])
+                send(rfirst.at[k, d], yfirst.at[k, d - 1], s2s, s2r.at[k], ypeer[d])
             return
         for i, at in entering(k):
             total = sums[k, 0, lines(i)]
@@ -312,10 +318,10 @@
         mark = onset_ref[h * vh : (h + 1) * vh, pl.ds(pl.multiple_of(at * LANES, LANES), LANES)]
         cos, sin = unit(mark)
         if k < early:
-            arrived(yfirst, s2r.at[k])
-            both = [[rfirst[0, f, i] for f in range(nf)] for i in range(2)]
+            arrived(yfirst.at[k], s2r.at[k])
+            both = [[rfirst[k, 0, f, i] for f in range(nf)] for i in range(2)]
             for d in range(1, ny):
-                both = [[both[i][f] + yfirst[d - 1, f, i] for f in range(nf)] for i in range(2)]
+                both = [[both[i][f] + yfirst[k, d - 1, f, i] for f in range(nf)] for i in range(2)]
             xr, xi = both
         else:
             arrived(rbuf.at[k, : nf - 1], s3r.at[k])
@@ -352,7 +358,7 @@
             if k < steps - late:
                 for d in range(1, ny):
                     send(at, at, s5s, s5r.at[k + sem, d - 1], ypeer[d])
-            send(at, at, s6s, s6r.at[lot(k), 0], partner)
+            send(at, at, s6s, s6r.at[ch, 0], partner)
 
     def stage_pass(k):
         ch, h = divmod(k, parts)
@@ -363,10 +369,7 @@
                     arrived(at, s5r.at[k + sem, d - 1])
                 else:
                     arrived(obuf.at[k, : nf - 1], s8r.at[d - 1])
-                send(at, at, s6s, s6r.at[lot(k), d], partner)
-
-    def lot(k):
-        return k // parts if k < (chunks - 1) * parts else chunks - 1 + k % parts
+                send(at, at, s6s, s6r.at[ch, d], partner)
 
     def load_block(b, hs):
         if aligned:
@@ -381,11 +384,7 @@
     def forward(ch, d, hs):
         j = ch * tiles + (y + ny - d) % ny
         there = block((y + ny - d) % ny, 1 - c, ch)
-        if ch < chunks - 1:
-            arrived(source.at[there], s6r.at[ch, d])
-        else:
-            for i in hs:
-                arrived(source.at[there, i], s6r.at[ch + i, d])
+        arrived(source.at[there], s6r.at[ch, d])
         h, l = split(lanes(*[load_block(j * blocks + b, hs) for b in range(blocks)]))
         rh = lanes(*[right_h[p, j] for p in range(panels)])
         rl = lanes(*[right_l[p, j] for p in range(panels)])
@@ -420,23 +419,16 @@
         for d in range(1, ny):
             forward(k // parts, d, list(range(parts)))
 
-    def stage_near(k):
-        forward(k // parts, 0, [k % parts])
-
-    def stage_far(k):
-        for d in range(1, ny):
-            forward(k // parts, d, [k % parts])
-
     assert blocks == 2
     run = {"adjoint": stage_adjoint, "sum": stage_sum, "out": stage_out, "gate": stage_gate, "back": stage_back,
-           "pass": stage_pass, "cross": stage_cross, "own": stage_own, "forward": stage_forward, "near": stage_near, "far": stage_far}
+           "pass": stage_pass, "cross": stage_cross, "own": stage_own, "forward": stage_forward}
     for stage, k in schedule(chunks, parts, late):
         run[stage](k)
     arrived(buf1, s1s)
     arrived(buf2, s2s)
     arrived(rbuf.at[early:, : nf - 1], s3s)
     if early:
-        arrived(rfirst.at[:, : nf - 1], s7s)
+        arrived(rfirst.at[:, :, : nf - 1], s7s)
     arrived(obuf.at[:, : nf - 1], s4s)
     arrived(buf2, s5s)
     if late:
@@ -448,12 +440,12 @@
     "adjoint": -8, "sum": -5.5, "out": 0, "gate": 2.5, "cross": 5.2, "back": 5.3, "pass": 6.3, "own": 6.4, "forward": 7.4,
 }
 ORDER = [
-    ("adjoint", 0), ("adjoint", 1), ("sum", 0), ("sum", 1), ("sum", 2), ("adjoint", 2), ("sum", 3), ("sum", 4),
-    ("sum", 5), ("out", 1), ("out", 2), ("out", 3), ("out", 0), ("adjoint", 3), ("out", 4), ("sum", 6), ("gate", 1),
-    ("sum", 7), ("out", 5), ("gate", 0), ("out", 6), ("gate", 3), ("out", 7), ("back", 1), ("gate", 2), ("gate", 5),
-    ("gate", 4), ("pass", 1), ("back", 0), ("back", 3), ("own", 1), ("gate", 6), ("gate", 7), ("back", 2),
-    ("back", 5), ("own", 3), ("cross", 7), ("pass", 3), ("back", 4), ("pass", 0), ("back", 6), ("pass", 2),
-    ("own", 5), ("forward", 1), ("back", 7), ("pass", 5), ("forward", 3), ("pass", 4), ("own", 7), ("pass", 7),
+    ("adjoint", 0), ("adjoint", 1), ("sum", 0), ("sum", 1), ("sum", 2), ("sum", 3), ("adjoint", 2), ("adjoint", 3),
+    ("sum", 4), ("sum", 5), ("out", 2), ("out", 3), ("out", 4), ("out", 0), ("sum", 6), ("sum", 7), ("out", 5),
+    ("gate", 2), ("out", 1), ("gate", 3), ("gate", 0), ("out", 6), ("out", 7), ("back", 2), ("back", 3), ("gate", 1),
+    ("back", 0), ("gate", 5), ("gate", 4), ("gate", 6), ("gate", 7), ("own", 3), ("back", 1), ("back", 5),
+    ("own", 1), ("back", 4), ("pass", 3), ("pass", 2), ("cross", 7), ("back", 6), ("pass", 0), ("own", 5),
+    ("pass", 1), ("forward", 3), ("back", 7), ("pass", 5), ("forward", 1), ("pass", 4), ("own", 7), ("pass", 7),
     ("pass", 6), ("forward", 5), ("forward", 7),
 ]
 
@@ -488,6 +480,7 @@
     vh = vp // parts
     steps = chunks * parts
     prow = pair // parts
+    early, late = (2, 1) if ny == 2 and steps > 2 + 1 else (0, 0)
     left = jnp.transpose(left_factors[0], (1, 0, 2))
     hbm = pl.BlockSpec(memory_space=pl.ANY)
     dma = lambda *n: pltpu.SemaphoreType.DMA(n) if n else pltpu.SemaphoreType.DMA
@@ -500,7 +493,7 @@
         kept = (panels, 2, virtual, rows)
     field_in, direct_in = shaped(wavefield[0]), shaped(direct[0])
     out = pl.pallas_call(
-        functools.partial(marchenko_kernel, nf, ny, chunks),
+        functools.partial(marchenko_kernel, nf, ny, chunks, early, late),
         in_specs=[hbm] * 6,
         out_specs=pl.BlockSpec(memory_space=pltpu.VMEM),
         out_shape=pltpu.VMEM(direct_in.shape, F32),
@@ -510,7 +503,7 @@
             pltpu.VMEM(kept, F32),
             pltpu.VMEM(kept, F32),
             [pltpu.VMEM((slots, rows, width), F32)] * panels,
-            pltpu.VMEM((panels, slots, rows, width), F32),
+            [pltpu.VMEM((slots, rows, width), F32)] * panels,
             pltpu.VMEM((panels, pair, 3 * rows), BF16),
             *split_buf,
             *split_buf,
@@ -523,15 +516,15 @@
             pltpu.VMEM((steps, nf, 2, vh, LANES), F32),
             pltpu.VMEM((blocks, parts, 2, nf, vh, LANES), F32),
             pltpu.VMEM((pair, LANES), F32),
-            pltpu.VMEM((ny, 2, nf, vh, LANES), F32),
-            pltpu.VMEM((ny, nf, 2, vh, LANES), F32),
-            pltpu.VMEM((ny - 1, nf, 2, vh, LANES), F32),
+            pltpu.VMEM((max(early, 1), ny, 2, nf, vh, LANES), F32),
+            pltpu.VMEM((max(early, 1), ny, nf, 2, vh, LANES), F32),
+            pltpu.VMEM((max(early, 1), ny - 1, nf, 2, vh, LANES), F32),
             pltpu.VMEM((ny - 1, nf, 2, vh, LANES), F32),
             dma(), dma(),
-            dma(panels), dma(), dma(panels), dma(),
+            dma(), dma(), dma(panels), dma(panels),
             dma(), dma(steps), dma(), dma(steps + 1), dma(), dma(steps),
-            dma(), dma(steps + 1), dma(), dma(steps + 1, ny - 1), dma(), dma(chunks - 1 + parts, ny),
-            dma(), dma(), dma(), dma(ny - 1),
+            dma(), dma(steps + 1), dma(), dma(steps + 1, ny - 1), dma(), dma(chunks, ny),
+            dma(), dma(max(early, 1)), dma(), dma(ny - 1),
         ],
         compiler_params=pltpu.CompilerParams(collective_id=0, has_side_effects=True),
         name="marchenko",

time: 43.6 us -> 43 us (0.986)
  Pallas kernels: 42.5 us -> 41.9 us
    pallas_call x1, Pallas kernels: 42.5 us -> 41.9 us  [shards(): pl.pallas_call(functools.partial(marchenko_kernel, nf, ny, chunks, early,...]
where the time goes in v3:
time: 43 us; the launch traced here: 42.9 us
  Pallas kernels  41.9 us (97%)
  local copies, waits for them, and re-layouts  0.97 us (2%)
    pallas_call x1, Pallas kernels, shards(): pl.pallas_call(functools.partial(marchenko_kernel, nf, ny, chunks, early,...  41.9 us
    unnamed x1, local copies, waits for them, and re-layouts  0.97 us

profile of v3, /device:TPU:1, one launch (start us, length us, event | category | flops | bytes accessed | tf_op | source)
XLA Modules:
  0.0 42.9 jit_solution(14036118722165407968)
XLA Ops:
  0.0 41.9 %marchenko.1 = f32[2,8,2,8,1024]{4,3,2,1,0:T(8,128)S(1)} custom-call(s32[4,6]{1,0:T(4,128)} %tile_hbm.1, s32[16,2048]{1,0:T(8,128)} %onset_hbm.1, f32[2,8,2,8,1024]{4,3,2,1,0:T(8,128)} %bitcast.10, f32[2,8,2,8,1024]{4,3,2,1,0:T(8,128)} %bitcast.11, f32[6,1024,128]{2,1,0:T(8,128)} %bitcast.8, f32[4,6,256,128]{3,2,1,0:T(8,128)} %bitcast.9), custom_call_target="tpu_custom_call" | custom-call | tf_op jit(solution)/shard_map/marchenko/pallas_call | solution.py:495
  41.9 1.0 %copy.8 = f32[1,2,128,1024]{3,2,1,0:T(8,128)} copy(f32[1,2,128,1024]{3,2,1,0:T(8,128)S(1)} %bitcast.7) | data formatting | bytes 2097152

commit v4 on v3

--- a/solution.py
+++ b/solution.py
@@ -371,59 +371,64 @@
                     arrived(obuf.at[k, : nf - 1], s8r.at[d - 1])
                 send(at, at, s6s, s6r.at[ch, d], partner)
 
-    def load_block(b, hs):
+    def load_block(b):
         if aligned:
-            return source[b, hs[0] : hs[-1] + 1].reshape(len(hs) * prow, LANES)
+            return source[b].reshape(pair, LANES)
         for i in range(2 * nf):
             chosen_ref[i * vh : (i + 1) * vh, :] = source[b, 0, i // nf, i % nf]
         return chosen_ref[...]
 
-    seen = [0] * parts
+    applied = []
     gates = []
 
-    def forward(ch, d, hs):
-        j = ch * tiles + (y + ny - d) % ny
-        there = block((y + ny - d) % ny, 1 - c, ch)
-        arrived(source.at[there], s6r.at[ch, d])
-        h, l = split(lanes(*[load_block(j * blocks + b, hs) for b in range(blocks)]))
-        rh = lanes(*[right_h[p, j] for p in range(panels)])
-        rl = lanes(*[right_l[p, j] for p in range(panels)])
-        products = mxu(lanes(h, h, l), jnp.concatenate([rh, rl, rh], axis=0), NN)
-        if not any(seen):
+    def apply(items):
+        found = []
+        for ch, d in items:
+            yy = (y + ny - d) % ny
+            j = ch * tiles + yy
+            arrived(source.at[block(yy, 1 - c, ch)], s6r.at[ch, d])
+            h, l = split(lanes(*[load_block(j * blocks + b) for b in range(blocks)]))
+            rh = lanes(*[right_h[p, j] for p in range(panels)])
+            rl = lanes(*[right_l[p, j] for p in range(panels)])
+            found.append((j, mxu(lanes(h, h, l), jnp.concatenate([rh, rl, rh], axis=0), NN)))
+        if not applied:
             arrived(direct, direct_sem)
-        for i in hs:
-            seen[i] += 1
+        applied.extend(items)
+        last = len(applied) == chunks * ny
         for p in range(panels):
-            ph, plow = split(coef_of(products[:, p * width : (p + 1) * width]))
-            lh, ll = left_h[p, j], left_l[p, j]
-            total = mxu(lanes(ph, ph, plow), lanes(lh, ll, lh), NT_DIMS)
-            for n, i in enumerate(hs):
-                mine = total[n * prow : (n + 1) * prow]
-                if not aligned:
-                    done = direct[p] - mine.reshape(direct.shape[1:])
-                    if seen[i] == chunks * ny:
-                        out_ref[:, :, p * rows : (p + 1) * rows] = done
-                    else:
-                        direct[p] = done
-                else:
-                    done = direct[p, i] - mine.reshape(direct.shape[2:])
-                    if seen[i] == chunks * ny:
-                        out_ref[:, :, i, :, p * rows : (p + 1) * rows] = done
-                    else:
-                        direct[p, i] = done
-
-    def stage_own(k):
-        forward(k // parts, 0, list(range(parts)))
-
-    def stage_forward(k):
-        for d in range(1, ny):
-            forward(k // parts, d, list(range(parts)))
+            ins, outs = [], []
+            for j, products in found:
+                ph, plow = split(coef_of(products[:, p * width : (p + 1) * width]))
+                lh, ll = left_h[p, j], left_l[p, j]
+                ins += [ph, ph, plow]
+                outs += [lh, ll, lh]
+            total = mxu(lanes(*ins), lanes(*outs), NT_DIMS)
+            done = direct[p] - total.reshape(direct.shape[1:])
+            if not last:
+                direct[p] = done
+            elif aligned:
+                for i in range(parts):
+                    out_ref[:, :, i, :, p * rows : (p + 1) * rows] = done[i]
+            else:
+                out_ref[:, :, p * rows : (p + 1) * rows] = done
+
+    def tiles_of(stage, k):
+        return [(k // parts, d) for d in (range(1) if stage == "own" else range(1, ny))]
 
     assert blocks == 2
     run = {"adjoint": stage_adjoint, "sum": stage_sum, "out": stage_out, "gate": stage_gate, "back": stage_back,
-           "pass": stage_pass, "cross": stage_cross, "own": stage_own, "forward": stage_forward}
-    for stage, k in schedule(chunks, parts, late):
-        run[stage](k)
+           "pass": stage_pass, "cross": stage_cross}
+    held = []
+    plan = schedule(chunks, parts, late)
+    for n, (stage, k) in enumerate(plan):
+        if stage in run:
+            run[stage](k)
+            continue
+        held += tiles_of(stage, k)
+        more = n + 2 < len(plan) and plan[n + 1][0] not in run
+        while held and (len(held) >= GROUP or not more):
+            apply(held[:GROUP])
+            del held[:GROUP]
     arrived(buf1, s1s)
     arrived(buf2, s2s)
     arrived(rbuf.at[early:, : nf - 1], s3s)
@@ -439,10 +444,11 @@
 LAGS = {
     "adjoint": -8, "sum": -5.5, "out": 0, "gate": 2.5, "cross": 5.2, "back": 5.3, "pass": 6.3, "own": 6.4, "forward": 7.4,
 }
+GROUP = 2
 ORDER = [
     ("adjoint", 0), ("adjoint", 1), ("sum", 0), ("sum", 1), ("sum", 2), ("sum", 3), ("adjoint", 2), ("adjoint", 3),
     ("sum", 4), ("sum", 5), ("out", 2), ("out", 3), ("out", 4), ("out", 0), ("sum", 6), ("sum", 7), ("out", 5),
-    ("gate", 2), ("out", 1), ("gate", 3), ("gate", 0), ("out", 6), ("out", 7), ("back", 2), ("back", 3), ("gate", 1),
+    ("gate", 2), ("out", 1), ("gate", 3), ("gate", 0), ("out", 6), ("out", 7), ("back", 2), ("gate", 1), ("back", 3),
     ("back", 0), ("gate", 5), ("gate", 4), ("gate", 6), ("gate", 7), ("own", 3), ("back", 1), ("back", 5),
     ("own", 1), ("back", 4), ("pass", 3), ("pass", 2), ("cross", 7), ("back", 6), ("pass", 0), ("own", 5),
     ("pass", 1), ("forward", 3), ("back", 7), ("pass", 5), ("forward", 1), ("pass", 4), ("own", 7), ("pass", 7),

time: 43 us -> 43 us (level)
  no operation moved by 1% of the time
where the time goes in v4:
time: 43 us; the launch traced here: 42.9 us
  Pallas kernels  41.9 us (97%)
  local copies, waits for them, and re-layouts  0.97 us (2%)
    pallas_call x1, Pallas kernels, shards(): pl.pallas_call(functools.partial(marchenko_kernel, nf, ny, chunks, early,...  41.9 us
    unnamed x1, local copies, waits for them, and re-layouts  0.97 us

profile of v4, /device:TPU:1, one launch (start us, length us, event | category | flops | bytes accessed | tf_op | source)
XLA Modules:
  0.0 42.9 jit_solution(18293870440263824685)
XLA Ops:
  0.0 41.9 %marchenko.1 = f32[2,8,2,8,1024]{4,3,2,1,0:T(8,128)S(1)} custom-call(s32[4,6]{1,0:T(4,128)} %tile_hbm.1, s32[16,2048]{1,0:T(8,128)} %onset_hbm.1, f32[2,8,2,8,1024]{4,3,2,1,0:T(8,128)} %bitcast.10, f32[2,8,2,8,1024]{4,3,2,1,0:T(8,128)} %bitcast.11, f32[6,1024,128]{2,1,0:T(8,128)} %bitcast.8, f32[4,6,256,128]{3,2,1,0:T(8,128)} %bitcast.9), custom_call_target="tpu_custom_call" | custom-call | tf_op jit(solution)/shard_map/marchenko/pallas_call | solution.py:501
  41.9 1.0 %copy.8 = f32[1,2,128,1024]{3,2,1,0:T(8,128)} copy(f32[1,2,128,1024]{3,2,1,0:T(8,128)S(1)} %bitcast.7) | data formatting | bytes 2097152

commit v5 on v4

--- a/solution.py
+++ b/solution.py
@@ -331,14 +331,14 @@
         for f in range(nf):
             obuf[k, f, 0] = br[f]
             obuf[k, f, 1] = bi[f]
+        if k >= steps - late:
+            for d in range(1, ny):
+                send(obuf.at[k], ylast.at[d - 1], s5s, s5r.at[k, d - 1], ypeer[d])
         for i, sem in leaving(k):
             for d in range(1, nf):
                 to = (me + d) % nf
                 send(obuf.at[k, to, i], source.at[at, h, i, me], s4s, s4r.at[k + sem], fpeer[d])
         source[at, h, :, me] = obuf[k, me]
-        if k >= steps - late:
-            for d in range(1, ny):
-                send(obuf.at[k], ylast.at[d - 1], s5s, s5r.at[k, d - 1], ypeer[d])
 
     def stage_cross(k):
         ch, h = divmod(k, parts)
@@ -529,7 +529,7 @@
             dma(), dma(),
             dma(), dma(), dma(panels), dma(panels),
             dma(), dma(steps), dma(), dma(steps + 1), dma(), dma(steps),
-            dma(), dma(steps + 1), dma(), dma(steps + 1, ny - 1), dma(), dma(chunks, ny),
+            dma(), dma(steps + 1 - late), dma(), dma(steps + 1 - late, ny - 1), dma(), dma(chunks, ny),
             dma(), dma(max(early, 1)), dma(), dma(ny - 1),
         ],
         compiler_params=pltpu.CompilerParams(collective_id=0, has_side_effects=True),

time: 43 us -> 43 us (level)
  no operation moved by 1% of the time
where the time goes in v5:
time: 43 us; the launch traced here: 42.8 us
  Pallas kernels  41.9 us (97%)
  local copies, waits for them, and re-layouts  0.97 us (2%)
    pallas_call x1, Pallas kernels, shards(): pl.pallas_call(functools.partial(marchenko_kernel, nf, ny, chunks, early,...  41.9 us
    unnamed x1, local copies, waits for them, and re-layouts  0.97 us

profile of v5, /device:TPU:1, one launch (start us, length us, event | category | flops | bytes accessed | tf_op | source)
XLA Modules:
  0.0 42.8 jit_solution(7970992209815903209)
XLA Ops:
  0.0 41.9 %marchenko.1 = f32[2,8,2,8,1024]{4,3,2,1,0:T(8,128)S(1)} custom-call(s32[4,6]{1,0:T(4,128)} %tile_hbm.1, s32[16,2048]{1,0:T(8,128)} %onset_hbm.1, f32[2,8,2,8,1024]{4,3,2,1,0:T(8,128)} %bitcast.10, f32[2,8,2,8,1024]{4,3,2,1,0:T(8,128)} %bitcast.11, f32[6,1024,128]{2,1,0:T(8,128)} %bitcast.8, f32[4,6,256,128]{3,2,1,0:T(8,128)} %bitcast.9), custom_call_target="tpu_custom_call" | custom-call | tf_op jit(solution)/shard_map/marchenko/pallas_call | solution.py:501
  41.9 1.0 %copy.8 = f32[1,2,128,1024]{3,2,1,0:T(8,128)} copy(f32[1,2,128,1024]{3,2,1,0:T(8,128)S(1)} %bitcast.7) | data formatting | bytes 2097152
